TPU v7x, 128 devices: a whole 4x4x4 slice. The times are simulated.
128 devices in a mesh: frames: 2 (over y_hi), codebook: 16 (over y_lo, x, core), hidden: 4 (over z).
Axes of the slice: x: 4, y: 4 (y_hi: 2, y_lo: 2; y = y_hi * 2 + y_lo), z: 4, core: 2. Of those that a mesh axis runs over, the one named last changes fastest.
Arguments:
- temporal: bfloat16 [4096, 4096], P(('frames', 'codebook'), 'hidden'), may hold values from -6 to 6
- frame_ids: int32 [4096, 16], P('frames', 'codebook'), may hold values from 0 to 2047
- proj_weight: bfloat16 [16, 4096, 1024], P('codebook', 'hidden'), may hold values from -0.09375 to 0.09375
- embed_table: bfloat16 [16, 2049, 1024], P('codebook'), may hold values from -6 to 6
- qkv_weight: bfloat16 [16, 3, 1024, 1024], P('codebook', None, None, 'hidden'), may hold values from -12 to 12
- out_weight: bfloat16 [16, 1024, 1024], P('codebook', 'hidden'), may hold values from -0.1875 to 0.1875
- gate_up: bfloat16 [16, 2, 1024, 4096], P('codebook', None, None, 'hidden'), may hold values from -0.1875 to 0.1875
- down_weight: bfloat16 [16, 4096, 1024], P('codebook', 'hidden'), may hold values from -0.09375 to 0.09375
- norm_gains: float32 [16, 2, 1024], P('codebook'), may hold values from 0.25 to 1.75
Outputs:
- depth_states: float32 [16, 4096, 1024], P('codebook', 'frames', 'hidden')
All inputs are finite; a program needn't handle non-finite values.
Results may differ from a plain program's by a relative error of at most 0.015.
Values may be sent and summed in bfloat16 or wider, within the bound.
A program may use at most 192 MiB of HBM per device.

v0:
```python
import jax
import jax.numpy as jnp
from jax import lax
from jax.sharding import PartitionSpec as P

HEADS = 16


def shifted(block, axis, distance):
    devices = range(lax.axis_size(axis))
    route = [(i - distance, i) for i in devices if i - distance in devices]
    return lax.ppermute(block, axis, route)


def normalize(values, norm_gain):
    return values * lax.rsqrt(jnp.mean(values * values, axis=-1, keepdims=True) + 1e-05) * norm_gain


def gated(normed, piece):
    gate_sum = jnp.dot(normed, piece[0], preferred_element_type=jnp.float32)
    upper_sum = jnp.dot(normed, piece[1], preferred_element_type=jnp.float32)
    return (jax.nn.silu(gate_sum) * upper_sum).astype(jnp.bfloat16)


def body(
    temporal,
    frame_ids,
    proj_weight,
    embed_table,
    qkv_weight,
    out_weight,
    gate_up,
    down_weight,
    norm_gains,
):
    code_index = lax.axis_index("codebook")
    hidden_index = lax.axis_index("hidden")
    hidden_count = lax.axis_size("hidden")
    start_id = embed_table.shape[1] - 1
    token_table = embed_table[0]
    norm_gain = norm_gains[0]
    earlier = shifted(frame_ids, "codebook", 1)[:, 0]
    previous = jnp.where(code_index == 0, start_id, earlier)
    partial_sum = jnp.dot(
        lax.all_gather(temporal, "codebook", axis=0, tiled=True),
        proj_weight[0],
        preferred_element_type=jnp.float32,
    )
    row_count = partial_sum.shape[0]
    x_zero = lax.psum(partial_sum.astype(jnp.bfloat16), "hidden").astype(jnp.float32) + token_table[
        previous
    ].astype(jnp.float32)
    normed = normalize(x_zero, norm_gain[0]).astype(jnp.bfloat16)
    local_width = qkv_weight.shape[3]
    local_heads = HEADS // hidden_count
    head_size = local_width // local_heads
    triple = jnp.einsum(
        "rd,kdc->krc", normed, qkv_weight[0], preferred_element_type=jnp.float32
    ).astype(jnp.bfloat16)
    query_heads = triple[0].reshape(row_count, local_heads, head_size)
    highest = jnp.full((row_count, local_heads), -1e30, jnp.float32)
    key_piece = lax.all_gather(triple[1][None], "codebook", axis=0, tiled=True)
    value_piece = lax.all_gather(triple[2][None], "codebook", axis=0, tiled=True)
    positions = key_piece.shape[0]
    key_heads = key_piece.reshape(positions, row_count, local_heads, head_size)
    value_heads = value_piece.reshape(positions, row_count, local_heads, head_size)
    scores = jnp.einsum(
        "fhd,jfhd->jfh", query_heads, key_heads, preferred_element_type=jnp.float32
    ) * head_size ** (-0.5)
    valid = (jnp.arange(positions, dtype=jnp.int32) <= code_index)[:, None, None]
    scores = jnp.where(valid, scores, -1e30)
    new_highest = jnp.maximum(highest, jnp.max(scores, axis=0))
    weights = jnp.where(valid, jnp.exp(scores - new_highest[None]), 0.0)
    running = jnp.sum(weights, axis=0)
    summed = jnp.einsum(
        "jfh,jfhd->fhd",
        weights.astype(jnp.bfloat16),
        value_heads,
        preferred_element_type=jnp.float32,
    )
    highest, running, summed = (new_highest, running, summed)
    attended = (summed / running[..., None]).reshape(row_count, local_width).astype(jnp.bfloat16)
    attention_part = jnp.dot(attended, out_weight[0], preferred_element_type=jnp.float32)
    residual = x_zero + lax.psum(attention_part.astype(jnp.bfloat16), "hidden").astype(jnp.float32)
    normed_two = normalize(residual, norm_gain[1]).astype(jnp.bfloat16)
    activated = gated(normed_two, gate_up[0])
    down_part = jnp.dot(activated, down_weight[0], preferred_element_type=jnp.float32)
    mlp_piece = lax.psum_scatter(
        down_part.astype(jnp.bfloat16), "hidden", scatter_dimension=1, tiled=True
    ).astype(jnp.float32)
    own_residual = lax.dynamic_slice_in_dim(residual, hidden_index * local_width, local_width, 1)
    return (own_residual + mlp_piece)[None]


def solution(mesh):
    placed = (
        P(("frames", "codebook"), "hidden"),
        P("frames", "codebook"),
        P("codebook", "hidden", None),
        P("codebook", None, None),
        P("codebook", None, None, "hidden"),
        P("codebook", "hidden", None),
        P("codebook", None, None, "hidden"),
        P("codebook", "hidden", None),
        P("codebook", None, None),
    )
    return jax.shard_map(
        body,
        mesh=mesh,
        in_specs=placed,
        out_specs=P("codebook", "frames", "hidden"),
        check_vma=False,
    )
```

profile of v0, /device:TPU:1, one launch (start us, length us, event | category | flops | bytes accessed | tf_op | source)
XLA Modules:
  0.0 563.1 jit_solution(17674491881883395552)
XLA Ops:
  7.3 42.5 %all-gather.4.cloned.1.call-done = bf16[2048,1024]{1,0:T(8,128)(2,1)} async-done(((bf16[128,1024]{1,0:T(8,128)(2,1)}), bf16[2048,1024]{1,0:T(8,128)(2,1)}) %all-gather.4.cloned.1.call-update) | async-done | bytes 4194320 | tf_op jit(solution)/shard_map/all_gather | solution.py:45
  49.8 8.3 %convolution_convert_fusion.2 = bf16[2048,1024]{1,0:T(8,128)(2,1)} fusion(bf16[2048,1024]{1,0:T(8,128)(2,1)} %all-gather.4.cloned.1.call-done, bf16[1,1024,1024]{2,1,0:T(8,128)(2,1)S(1)} %copy-done), kind=kOutput, calls=%fused_computation.16 | convolution fusion | flops 4297064448 | bytes 10485760 | tf_op jit(solution)/shard_map/dot_general | solution.py:44
  58.9 2.8 collective-permute-start
  62.5 13.8 %gather_fusion = bf16[2048,1024]{1,0:T(8,128)(2,1)} fusion(bf16[2049,1024]{1,0:T(8,128)(2,1)} %bitcast.66, s32[2048]{0:T(1024)S(1)} %broadcast_clamp_fusion), kind=kCustom, calls=%fused_computation | custom fusion | bytes 8396800 | tf_op jit(solution)/shard_map/gather | solution.py:50
  76.3 74.6 %all-reduce.3.cloned.1.call-done = bf16[2048,1024]{1,0:T(8,128)(2,1)} async-done(((bf16[2048,1024]{1,0:T(8,128)(2,1)}), bf16[2048,1024]{1,0:T(8,128)(2,1)}) %all-reduce.3.cloned.1.call-update) | async-done | bytes 4194320 | tf_op jit(solution)/shard_map/psum | solution.py:50
  150.9 5.0 multiply_reduce_fusion.3
  156.0 0.9 copy-done.3
  156.8 4.2 fusion.8
  161.3 1.3 copy.21
  162.7 1.3 copy.23
  164.6 90.1 %all-gather.6.cloned.1.call-done = bf16[16,2048,256]{2,1,0:T(8,128)(2,1)} async-done(((bf16[1,2048,256]{2,1,0:T(8,128)(2,1)}), bf16[16,2048,256]{2,1,0:T(8,128)(2,1)}) %all-gather.6.cloned.1.call-update) | async-done | bytes 16777232 | tf_op jit(solution)/shard_map/all_gather | solution.py:62
  254.7 22.0 %copy.40 = bf16[16,2048,256]{1,2,0:T(8,128)(2,1)} copy(bf16[16,2048,256]{2,1,0:T(8,128)(2,1)} %all-gather.6.cloned.1.call-done) | data formatting | bytes 33554432
  276.7 7.9 %multiply_reduce_fusion.1 = f32[2048,4,16]{0,1,2:T(4,128)S(1)} fusion(f32[2048,4,64]{0,2,1:T(8,128)S(1)} %convert.1, bf16[16,2048,256]{1,2,0:T(8,128)(2,1)} %copy.40), kind=kLoop, calls=%fused_computation.2 | loop fusion | flops 25034752 | bytes 19398656
  285.8 62.8 %all-gather.8.cloned.1.call-done = bf16[16,2048,256]{2,1,0:T(8,128)(2,1)} async-done(((bf16[1,2048,256]{2,1,0:T(8,128)(2,1)}), bf16[16,2048,256]{2,1,0:T(8,128)(2,1)}) %all-gather.8.cloned.1.call-update) | async-done | bytes 16777232 | tf_op jit(solution)/shard_map/all_gather | solution.py:63
  348.6 21.7 %copy.41 = bf16[16,2048,256]{1,2,0:T(8,128)(2,1)} copy(bf16[16,2048,256]{2,1,0:T(8,128)(2,1)} %all-gather.8.cloned.1.call-done) | data formatting | bytes 33554432
  370.3 7.7 %multiply_reduce_fusion = f32[2048,4,64]{0,2,1:T(8,128)S(1)} fusion(bf16[2048,4,16,64]{0,3,1,2:T(8,128)(2,1)} %bitcast.67, f32[2048,4,16]{0,1,2:T(4,128)S(1)} %copy.43), kind=kLoop, calls=%fused_computation.1 | loop fusion | flops 24641536 | bytes 19398656 | tf_op jit(solution)/shard_map/jfh,jfhd->fhd/dot_general | solution.py:75
  378.1 3.3 convolution_convert_fusion
  381.5 93.4 %all-reduce.5.cloned.1.call-done = bf16[2048,1024]{1,0:T(8,128)(2,1)} async-done(((bf16[2048,1024]{1,0:T(8,128)(2,1)}), bf16[2048,1024]{1,0:T(8,128)(2,1)}) %all-reduce.5.cloned.1.call-update) | async-done | bytes 4194320 | tf_op jit(solution)/shard_map/psum | solution.py:84
  474.9 5.8 %multiply_reduce_fusion.2 = (f32[2048]{0:T(1024)S(1)}, f32[2048,1024]{1,0:T(8,128)S(1)}) fusion(bf16[2048,1024]{1,0:T(8,128)(2,1)} %all-reduce.5.cloned.1.call-done, bf16[2048,1024]{1,0:T(8,128)(2,1)} %gather_fusion, bf16[2048,1024]{1,0:T(8,128)(2,1)} %all-reduce.3.cloned.1.call-done), kind=kLoop, calls=%fused_computation.5 | loop fusion | flops 14678016 | bytes 20979712 | tf_op jit(solution)/shard_map/reduce_sum | solution.py:16
  480.7 3.2 copy-done.4
  483.9 6.7 %fusion.14 = f32[2048,1024]{1,0:T(8,128)} fusion(bf16[1,2,1024,1024]{3,2,1,0:T(8,128)(2,1)S(1)} %copy-done.7, f32[2048,1024]{1,0:T(8,128)S(1)} %get-tuple-element.6, f32[1024]{0:T(1024)S(1)} %bitcast.71, f32[2048]{0:T(1024)S(1)} %add_rsqrt_fusion), kind=kOutput, calls=%fused_computation.21 | convolution fusion | flops 4301258752 | bytes 18886656 | tf_op jit(solution)/shard_map/dot_general | solution.py:20
  490.6 15.1 %convolution_convert_fusion.1 = bf16[2048,1024]{1,0:T(8,128)(2,1)} fusion(f32[2048,1024]{1,0:T(8,128)} %fusion.14, bf16[1,1024,1024]{2,1,0:T(8,128)(2,1)} %param.16, bf16[1,2,1024,1024]{3,2,1,0:T(8,128)(2,1)} %param.15, f32[2048,1024]{1,0:T(8,128)} %copy-done.4, f32[1024]{0:T(1024)S(1)} %bitcast.72, f32[2048]{0:T(1024)S(1)} %add_rsqrt_fusion), kind=kOutput, calls=%fused_computation.15 | convolution fusion | flops 8610906112 | bytes 25178112 | tf_op jit(solution)/shard_map/dot_general | solution.py:87
  505.8 47.0 %reduce-scatter.2.cloned.1.call-done = bf16[2048,256]{1,0:T(8,128)(2,1)} async-done(((bf16[2048,1024]{1,0:T(8,128)(2,1)}), bf16[2048,256]{1,0:T(8,128)(2,1)}) %reduce-scatter.2.cloned.1.call-update) | async-done | bytes 1048592 | tf_op jit(solution)/shard_map/reduce_scatter | solution.py:88
  552.9 3.4 add_bitcast_fusion
  (44 shorter events, 4.6 us)
Async XLA Ops:
  6.5 43.3 %copy-start = (bf16[1,1024,1024]{2,1,0:T(8,128)(2,1)S(1)}, bf16[1,1024,1024]{2,1,0:T(8,128)(2,1)}, u32[]{:S(2)}) copy-start(bf16[1,1024,1024]{2,1,0:T(8,128)(2,1)} %param.11) | copy-start | bytes 6291460
  6.5 43.3 %all-gather.4.cloned.1.call-start = ((), (), s32[]{:S(2)}) async-start(), calls=%async_computation.1 | async-start | bytes 4456448 | tf_op jit(solution)/shard_map/all_gather | solution.py:45
  7.3 143.6 %all-reduce.3.cloned.1.call-start = ((), (), s32[]{:S(2)}) async-start(), calls=%async_computation.2 | async-start | bytes 8388608 | tf_op jit(solution)/shard_map/psum | solution.py:50
  58.2 0.7 copy-start.9
  58.2 3.5 copy-start.6
  58.2 196.5 %all-gather.6.cloned.1.call-start = ((), (), s32[]{:S(2)}) async-start(), calls=%async_computation.3 | async-start | bytes 17825792 | tf_op jit(solution)/shard_map/all_gather | solution.py:62
  58.9 3.6 collective-permute-start
  62.5 93.4 %copy-start.8 = (bf16[1,3,1024,256]{3,2,1,0:T(8,128)(2,1)S(1)}, bf16[1,3,1024,256]{3,2,1,0:T(8,128)(2,1)}, u32[]{:S(2)}) copy-start(bf16[1,3,1024,256]{3,2,1,0:T(8,128)(2,1)} %param.13) | copy-start | bytes 4718596
  150.9 5.1 copy-start.2
  150.9 5.9 %copy-start.3 = (bf16[2048,1024]{1,0:T(8,128)(2,1)S(1)}, bf16[2048,1024]{1,0:T(8,128)(2,1)}, u32[]{:S(2)}) copy-start(bf16[2048,1024]{1,0:T(8,128)(2,1)} %all-reduce.3.cloned.1.call-done) | copy-start | bytes 12582916
  162.7 185.9 %all-gather.8.cloned.1.call-start = ((), (), s32[]{:S(2)}) async-start(), calls=%async_computation.4 | async-start | bytes 17825792 | tf_op jit(solution)/shard_map/all_gather | solution.py:63
  164.1 310.8 %all-reduce.5.cloned.1.call-start = ((), (), s32[]{:S(2)}) async-start(), calls=%async_computation.5 | async-start | bytes 8388608 | tf_op jit(solution)/shard_map/psum | solution.py:84
  370.3 7.9 %copy-start.5 = (bf16[1,256,1024]{2,1,0:T(8,128)(2,1)S(1)}, bf16[1,256,1024]{2,1,0:T(8,128)(2,1)}, u32[]{:S(2)}) copy-start(bf16[1,256,1024]{2,1,0:T(8,128)(2,1)} %param.14) | copy-start | bytes 1572868
  381.4 171.4 %reduce-scatter.2.cloned.1.call-start = ((), (), s32[]{:S(2)}) async-start(), calls=%async_computation.6 | async-start | bytes 5242880 | tf_op jit(solution)/shard_map/reduce_scatter | solution.py:88
  474.9 9.1 %copy-start.7 = (bf16[1,2,1024,1024]{3,2,1,0:T(8,128)(2,1)S(1)}, bf16[1,2,1024,1024]{3,2,1,0:T(8,128)(2,1)}, u32[]{:S(2)}) copy-start(bf16[1,2,1024,1024]{3,2,1,0:T(8,128)(2,1)} %param.15) | copy-start | bytes 12582916
  480.7 3.2 copy-start.4
  505.8 50.5 %copy-start.1 = (bf16[1,1024,1024]{2,1,0:T(8,128)(2,1)S(1)}, bf16[1,1024,1024]{2,1,0:T(8,128)(2,1)}, u32[]{:S(2)}) copy-start(bf16[1,1024,1024]{2,1,0:T(8,128)(2,1)} %param.11) | copy-start | bytes 6291460
Sparse Core Ops, SparseCore 0:
  9.0 40.7 all-gather.3
  58.3 92.5 all-reduce.2
  162.8 91.8 all-gather.5
  256.2 92.3 all-gather.7
  381.6 93.2 all-reduce.4
  505.9 46.8 reduce-scatter.1
where the time goes:
time: 564 us; the launch traced here: 563 us
  waiting for transfers between devices  412 us (73%)
  local copies, waits for them, and re-layouts  65.5 us (12%)
  matrix products  37.6 us (7%)
  other arithmetic  31.1 us (6%)
  between operations  13.7 us (2%)
    psum x1, waiting for transfers between devices, body(): lax.psum(attention_part.astype(jnp.bfloat16), 'hidden').astype(jnp.float32)  93.4 us
    all_gather x1, waiting for transfers between devices, body(): key_piece = lax.all_gather(triple[1][None], 'codebook', axis=0, tiled=True)  90.1 us
    psum x1, waiting for transfers between devices, body(): lax.psum(partial_sum.astype(jnp.bfloat16), 'hidden').astype(jnp.float32)  74.6 us
    all_gather x1, waiting for transfers between devices, body(): lax.all_gather(triple[2][None], 'codebook', axis=0, tiled=True)  62.8 us
    unnamed x23, local copies, waits for them, and re-layouts  48.7 us
    reduce_scatter x1, waiting for transfers between devices, body(): lax.psum_scatter(down_part.astype(jnp.bfloat16), 'hidden', scatter_dimens...  47 us
    all_gather x1, waiting for transfers between devices, body(): lax.all_gather(temporal, 'codebook', axis=0, tiled=True)  42.5 us
    dot_general x1, matrix products, body(): jnp.dot(activated, down_weight[0], preferred_element_type=jnp.float32)  15.1 us
  transfers between devices with their start and end apart: 7, of which 7 were waited for; matrix products, arithmetic and copies ran while one was open for 8% of the time, Pallas kernels for 0%

commit v1 on v0

--- a/solution.py
+++ b/solution.py
@@ -81,7 +81,9 @@
     highest, running, summed = (new_highest, running, summed)
     attended = (summed / running[..., None]).reshape(row_count, local_width).astype(jnp.bfloat16)
     attention_part = jnp.dot(attended, out_weight[0], preferred_element_type=jnp.float32)
-    residual = x_zero + lax.psum(attention_part.astype(jnp.bfloat16), "hidden").astype(jnp.float32)
+    residual = x_zero + jnp.sum(
+        lax.all_gather(attention_part.astype(jnp.bfloat16), "hidden"), axis=0
+    ).astype(jnp.float32)
     normed_two = normalize(residual, norm_gain[1]).astype(jnp.bfloat16)
     activated = gated(normed_two, gate_up[0])
     down_part = jnp.dot(activated, down_weight[0], preferred_element_type=jnp.float32)

time: 564 us -> 639 us (1.13)
  waiting for transfers between devices: 412 us -> 474 us
  other arithmetic: 31.1 us -> 43.2 us
    all_gather x0 -> x1, waiting for transfers between devices: none -> 154 us  [body(): lax.all_gather(attention_part.astype(jnp.bfloat16), 'hidden')]
    psum x1 -> x0, waiting for transfers between devices: 93.4 us -> none  [body(): lax.psum(attention_part.astype(jnp.bfloat16), 'hidden').astype(jnp.float32)]
    reduce_sum x0 -> x1, other arithmetic: none -> 12.1 us  [body(): jnp.sum(lax.all_gather(attention_part.astype(jnp.bfloat16), 'hidden'), ax...]
  transfers between devices with their start and end apart: 7 -> 7, of which waited for: 7 -> 7; matrix products, arithmetic and copies ran while one was open for 8% -> 7% of each run, Pallas kernels for 0% -> 0%
where the time goes in v1:
time: 639 us; the launch traced here: 637 us
  waiting for transfers between devices  474 us (74%)
  local copies, waits for them, and re-layouts  65.5 us (10%)
  other arithmetic  43.2 us (7%)
  matrix products  37.6 us (6%)
  between operations  13.7 us (2%)
    all_gather x1, waiting for transfers between devices, body(): lax.all_gather(attention_part.astype(jnp.bfloat16), 'hidden')  154 us
    all_gather x1, waiting for transfers between devices, body(): key_piece = lax.all_gather(triple[1][None], 'codebook', axis=0, tiled=True)  90.1 us
    psum x1, waiting for transfers between devices, body(): lax.psum(partial_sum.astype(jnp.bfloat16), 'hidden').astype(jnp.float32)  74.6 us
    all_gather x1, waiting for transfers between devices, body(): lax.all_gather(triple[2][None], 'codebook', axis=0, tiled=True)  62.8 us
    unnamed x23, local copies, waits for them, and re-layouts  48.7 us
    reduce_scatter x1, waiting for transfers between devices, body(): lax.psum_scatter(down_part.astype(jnp.bfloat16), 'hidden', scatter_dimens...  48.2 us
    all_gather x1, waiting for transfers between devices, body(): lax.all_gather(temporal, 'codebook', axis=0, tiled=True)  42.5 us
    dot_general x1, matrix products, body(): jnp.dot(activated, down_weight[0], preferred_element_type=jnp.float32)  15.1 us
  transfers between devices with their start and end apart: 7, of which 7 were waited for; matrix products, arithmetic and copies ran while one was open for 7% of the time, Pallas kernels for 0%

profile of v1, /device:TPU:1, one launch (start us, length us, event | category | flops | bytes accessed | tf_op | source)
XLA Modules:
  0.0 637.4 jit_solution(15942974898449882378)
XLA Ops:
  7.3 42.5 %all-gather.6.cloned.1.call-done = bf16[2048,1024]{1,0:T(8,128)(2,1)} async-done(((bf16[128,1024]{1,0:T(8,128)(2,1)}), bf16[2048,1024]{1,0:T(8,128)(2,1)}) %all-gather.6.cloned.1.call-update) | async-done | bytes 4194320 | tf_op jit(solution)/shard_map/all_gather | solution.py:45
  49.8 8.3 %convolution_convert_fusion.2 = bf16[2048,1024]{1,0:T(8,128)(2,1)} fusion(bf16[2048,1024]{1,0:T(8,128)(2,1)} %all-gather.6.cloned.1.call-done, bf16[1,1024,1024]{2,1,0:T(8,128)(2,1)S(1)} %copy-done), kind=kOutput, calls=%fused_computation.16 | convolution fusion | flops 4297064448 | bytes 10485760 | tf_op jit(solution)/shard_map/dot_general | solution.py:44
  58.9 2.8 collective-permute-start
  62.5 13.8 %gather_fusion = bf16[2048,1024]{1,0:T(8,128)(2,1)} fusion(bf16[2049,1024]{1,0:T(8,128)(2,1)} %bitcast.67, s32[2048]{0:T(1024)S(1)} %broadcast_clamp_fusion), kind=kCustom, calls=%fused_computation | custom fusion | bytes 8396800 | tf_op jit(solution)/shard_map/gather | solution.py:50
  76.3 74.6 %all-reduce.2.cloned.1.call-done = bf16[2048,1024]{1,0:T(8,128)(2,1)} async-done(((bf16[2048,1024]{1,0:T(8,128)(2,1)}), bf16[2048,1024]{1,0:T(8,128)(2,1)}) %all-reduce.2.cloned.1.call-update) | async-done | bytes 4194320 | tf_op jit(solution)/shard_map/psum | solution.py:50
  150.9 5.0 multiply_reduce_fusion.3
  156.8 4.2 fusion.8
  161.3 1.3 copy.21
  162.7 1.3 copy.23
  164.6 90.1 %all-gather.8.cloned.1.call-done = bf16[16,2048,256]{2,1,0:T(8,128)(2,1)} async-done(((bf16[1,2048,256]{2,1,0:T(8,128)(2,1)}), bf16[16,2048,256]{2,1,0:T(8,128)(2,1)}) %all-gather.8.cloned.1.call-update) | async-done | bytes 16777232 | tf_op jit(solution)/shard_map/all_gather | solution.py:62
  254.7 22.0 %copy.40 = bf16[16,2048,256]{1,2,0:T(8,128)(2,1)} copy(bf16[16,2048,256]{2,1,0:T(8,128)(2,1)} %all-gather.8.cloned.1.call-done) | data formatting | bytes 33554432
  276.7 7.9 %multiply_reduce_fusion.1 = f32[2048,4,16]{0,1,2:T(4,128)S(1)} fusion(f32[2048,4,64]{0,2,1:T(8,128)S(1)} %convert.2, bf16[16,2048,256]{1,2,0:T(8,128)(2,1)} %copy.40), kind=kLoop, calls=%fused_computation.2 | loop fusion | flops 25034752 | bytes 19398656
  285.8 62.8 %all-gather.10.cloned.1.call-done = bf16[16,2048,256]{2,1,0:T(8,128)(2,1)} async-done(((bf16[1,2048,256]{2,1,0:T(8,128)(2,1)}), bf16[16,2048,256]{2,1,0:T(8,128)(2,1)}) %all-gather.10.cloned.1.call-update) | async-done | bytes 16777232 | tf_op jit(solution)/shard_map/all_gather | solution.py:63
  348.6 21.7 %copy.41 = bf16[16,2048,256]{1,2,0:T(8,128)(2,1)} copy(bf16[16,2048,256]{2,1,0:T(8,128)(2,1)} %all-gather.10.cloned.1.call-done) | data formatting | bytes 33554432
  370.3 7.7 %multiply_reduce_fusion = f32[2048,4,64]{0,2,1:T(8,128)S(1)} fusion(bf16[2048,4,16,64]{0,3,1,2:T(8,128)(2,1)} %bitcast.68, f32[2048,4,16]{0,1,2:T(4,128)S(1)} %copy.43), kind=kLoop, calls=%fused_computation.1 | loop fusion | flops 24641536 | bytes 19398656 | tf_op jit(solution)/shard_map/jfh,jfhd->fhd/dot_general | solution.py:75
  378.1 3.2 convolution_convert_fusion
  381.7 154.2 %all-gather.12.cloned.1.call-done = bf16[8192,1024]{1,0:T(8,128)(2,1)} async-done(((bf16[2048,1024]{1,0:T(8,128)(2,1)}), bf16[8192,1024]{1,0:T(8,128)(2,1)}) %all-gather.12.cloned.1.call-update) | async-done | bytes 16777232 | tf_op jit(solution)/shard_map/all_gather | solution.py:85
  535.9 12.1 %reduce_sum.41 = bf16[2048,1024]{1,0:T(8,128)(2,1)} reduce(bf16[4,2048,1024]{2,1,0:T(8,128)(2,1)} %bitcast.69, bf16[]{:T(256)} %constant.35.clone.1), dimensions={0}, to_apply=%region_4.5 | reduce | flops 6291456 | bytes 20971522 | tf_op jit(solution)/shard_map/reduce_sum | solution.py:84
  547.9 5.8 multiply_reduce_fusion.2
  553.8 3.2 copy-done.4
  557.0 6.8 %fusion.14 = f32[2048,1024]{1,0:T(8,128)} fusion(bf16[1,2,1024,1024]{3,2,1,0:T(8,128)(2,1)S(1)} %copy-done.7, f32[2048,1024]{1,0:T(8,128)S(1)} %get-tuple-element.6, f32[1024]{0:T(1024)S(1)} %bitcast.73, f32[2048]{0:T(1024)S(1)} %add_rsqrt_fusion), kind=kOutput, calls=%fused_computation.21 | convolution fusion | flops 4301258752 | bytes 18886656 | tf_op jit(solution)/shard_map/dot_general | solution.py:20
  563.7 15.1 %convolution_convert_fusion.1 = bf16[2048,1024]{1,0:T(8,128)(2,1)} fusion(f32[2048,1024]{1,0:T(8,128)} %fusion.14, bf16[1,1024,1024]{2,1,0:T(8,128)(2,1)} %param.16, bf16[1,2,1024,1024]{3,2,1,0:T(8,128)(2,1)} %param.15, f32[2048,1024]{1,0:T(8,128)} %copy-done.4, f32[1024]{0:T(1024)S(1)} %bitcast.74, f32[2048]{0:T(1024)S(1)} %add_rsqrt_fusion), kind=kOutput, calls=%fused_computation.15 | convolution fusion | flops 8610906112 | bytes 25178112 | tf_op jit(solution)/shard_map/dot_general | solution.py:89
  578.9 48.2 %reduce-scatter.2.cloned.1.call-done = bf16[2048,256]{1,0:T(8,128)(2,1)} async-done(((bf16[2048,1024]{1,0:T(8,128)(2,1)}), bf16[2048,256]{1,0:T(8,128)(2,1)}) %reduce-scatter.2.cloned.1.call-update) | async-done | bytes 1048592 | tf_op jit(solution)/shard_map/reduce_scatter | solution.py:90
  627.2 3.4 add_bitcast_fusion
  (45 shorter events, 5.7 us)
Async XLA Ops:
  6.5 43.3 %copy-start = (bf16[1,1024,1024]{2,1,0:T(8,128)(2,1)S(1)}, bf16[1,1024,1024]{2,1,0:T(8,128)(2,1)}, u32[]{:S(2)}) copy-start(bf16[1,1024,1024]{2,1,0:T(8,128)(2,1)} %param.11) | copy-start | bytes 6291460
  6.5 43.3 %all-gather.6.cloned.1.call-start = ((), (), s32[]{:S(2)}) async-start(), calls=%async_computation.1 | async-start | bytes 4456448 | tf_op jit(solution)/shard_map/all_gather | solution.py:45
  7.3 143.6 %all-reduce.2.cloned.1.call-start = ((), (), s32[]{:S(2)}) async-start(), calls=%async_computation.2 | async-start | bytes 8388608 | tf_op jit(solution)/shard_map/psum | solution.py:50
  58.2 0.7 copy-start.9
  58.2 3.5 copy-start.6
  58.2 196.5 %all-gather.8.cloned.1.call-start = ((), (), s32[]{:S(2)}) async-start(), calls=%async_computation.3 | async-start | bytes 17825792 | tf_op jit(solution)/shard_map/all_gather | solution.py:62
  58.9 3.6 collective-permute-start
  62.5 93.4 %copy-start.8 = (bf16[1,3,1024,256]{3,2,1,0:T(8,128)(2,1)S(1)}, bf16[1,3,1024,256]{3,2,1,0:T(8,128)(2,1)}, u32[]{:S(2)}) copy-start(bf16[1,3,1024,256]{3,2,1,0:T(8,128)(2,1)} %param.13) | copy-start | bytes 4718596
  150.9 5.1 copy-start.2
  150.9 5.9 copy-start.3
  162.7 185.9 %all-gather.10.cloned.1.call-start = ((), (), s32[]{:S(2)}) async-start(), calls=%async_computation.4 | async-start | bytes 17825792 | tf_op jit(solution)/shard_map/all_gather | solution.py:63
  164.1 371.8 %all-gather.12.cloned.1.call-start = ((), (), s32[]{:S(2)}) async-start(), calls=%async_computation.6 | async-start | bytes 20971520 | tf_op jit(solution)/shard_map/all_gather | solution.py:85
  370.3 7.9 %copy-start.5 = (bf16[1,256,1024]{2,1,0:T(8,128)(2,1)S(1)}, bf16[1,256,1024]{2,1,0:T(8,128)(2,1)}, u32[]{:S(2)}) copy-start(bf16[1,256,1024]{2,1,0:T(8,128)(2,1)} %param.14) | copy-start | bytes 1572868
  381.4 245.8 %reduce-scatter.2.cloned.1.call-start = ((), (), s32[]{:S(2)}) async-start(), calls=%async_computation.5 | async-start | bytes 5242880 | tf_op jit(solution)/shard_map/reduce_scatter | solution.py:90
  547.9 9.1 %copy-start.7 = (bf16[1,2,1024,1024]{3,2,1,0:T(8,128)(2,1)S(1)}, bf16[1,2,1024,1024]{3,2,1,0:T(8,128)(2,1)}, u32[]{:S(2)}) copy-start(bf16[1,2,1024,1024]{3,2,1,0:T(8,128)(2,1)} %param.15) | copy-start | bytes 12582916
  553.8 3.2 copy-start.4
  578.9 51.7 %copy-start.1 = (bf16[1,1024,1024]{2,1,0:T(8,128)(2,1)S(1)}, bf16[1,1024,1024]{2,1,0:T(8,128)(2,1)}, u32[]{:S(2)}) copy-start(bf16[1,1024,1024]{2,1,0:T(8,128)(2,1)} %param.11) | copy-start | bytes 6291460
Sparse Core Ops, SparseCore 0:
  9.0 40.7 all-gather.5
  58.3 92.5 all-reduce.1
  162.8 91.8 all-gather.7
  256.2 92.3 all-gather.9
  381.5 154.2 all-gather.11
  579.0 48.0 reduce-scatter.1
